TPU v7x, 32 devices: a whole 2x2x4 slice. The times are simulated.
32 devices in a mesh: blk: 8 (over y, x, core), line: 4 (over z).
Axes of the slice: x: 2, y: 2, z: 4, core: 2. Of those that a mesh axis runs over, the one named last changes fastest.
Arguments:
- state: bfloat16 [32, 88, 256, 128], P('blk', None, 'line'), may hold values from -6 to 6
- speed_in: float32 [32, 256, 128], P('blk', 'line'), may hold values from -1 to 1
- speed_wall: float32 [32, 256, 128], P('blk', 'line'), may hold values from -1 to 1
- density: float32 [32, 256, 128], P('blk', 'line'), may hold values from 0.3 to 3
- rates: bfloat16 [88, 88], replicated, may hold values from -0.625 to 0.625
- wall_op: bfloat16 [256, 256], replicated, may hold values from -0.375 to 0.375
- block_perm: int32 [32], replicated, may hold values from 0 to 31, each once
- patch_src: int32 [32, 2, 16], P('blk', None, 'line'), may hold values from 0 to 63
- patch_flip: int32 [32, 2, 16], P('blk', None, 'line'), may hold values 0 or 1
- patch_wall: int32 [32, 2, 16], P('blk', None, 'line'), may hold values 0 or 1
Outputs:
- next_state: bfloat16 [32, 88, 256, 128], P('blk', None, 'line')
Inputs may be any that keep to these rules, and one draw needn't show every extreme that they name: `block_perm`: each block id 0 to 31 stands in exactly one slot. patch_src // 2 is a block id (not a slot) and patch_src % 2 its face; a patch's rows are the same rows of the source face. `patch_flip`: 1 reverses the order of a patch's rows. `patch_wall`: 1 mirrors the face's own cells in place of a neighbour's.
All inputs are finite; a program needn't handle non-finite values. No bound on the sum of `patch_flip` or of `patch_wall` on one device may be relied on, other than what follows from the above.
Results may differ from a plain program's by a relative error of at most 0.0014.
Values may be sent and summed in bfloat16 or wider, within the bound.
No kernel may reach another device: no remote copies, remote signals or barrier semaphores. Data moves between devices by JAX's collectives and lax.ppermute only.
A program may use at most 192 MiB of HBM per device.

v0:
```python
import math
import jax
import jax.numpy as jnp
from jax import lax
from jax.sharding import PartitionSpec as P

filter_sigma = 0.5
section_step = 0.25
deriv_coef = [5.0 / 6.0, -5.0 / 21.0, 5.0 / 84.0, -5.0 / 504.0, 1.0 / 1260.0]
high_pass = [(-1) ** offset * math.comb(10, 5 + offset) / 1024.0 for offset in range(-5, 6)]


def edge_cells(field):
    columns = field.shape[-1]
    return jnp.stack([field[..., :5], jnp.flip(field[..., columns - 5 :], -1)], 1)


def source_faces(block_perm, patch_src, patch_wall, first_slot):
    nblocks = block_perm.shape[0]
    block_ids = jnp.arange(nblocks, dtype=jnp.int32)
    matches = block_perm[None, :] == block_ids[:, None]
    slot_of = jnp.sum(jnp.where(matches, block_ids[None, :], 0), axis=1)
    owned = patch_src.shape[0]
    own_face = (first_slot + jnp.arange(owned, dtype=jnp.int32))[:, None, None] * 2 + jnp.arange(
        2, dtype=jnp.int32
    )[None, :, None]
    remote = jnp.take(slot_of, patch_src // 2) * 2 + patch_src % 2
    return jnp.where(patch_wall == 1, own_face, remote)


def select_ghosts(gathered, source, flips, patch_count):
    total = gathered.shape[0]
    chans = gathered.shape[2]
    rows = gathered.shape[3]
    flat = gathered.reshape(total * 2, chans, patch_count, rows // patch_count, 5)
    patch_index = jnp.arange(patch_count, dtype=jnp.int32)[None, None, :]
    picked = flat[source, :, patch_index]
    picked = jnp.where(flips[..., None, None, None] == 1, jnp.flip(picked, -2), picked)
    picked = jnp.transpose(picked, (0, 1, 3, 2, 4, 5))
    return picked.reshape(source.shape[0], 2, chans, rows, 5)


def section_update(state, ghosts, normal, speed_in, speed_wall, density, rates):
    values = state.astype(jnp.float32)
    columns = values.shape[-1]
    extended = jnp.concatenate(
        [jnp.flip(ghosts[:, 0].astype(jnp.float32), -1), values, ghosts[:, 1].astype(jnp.float32)],
        -1,
    )
    smooth = values
    for offset in range(11):
        smooth = (
            smooth - filter_sigma * high_pass[offset] * extended[..., offset : offset + columns]
        )
    slope = jnp.zeros_like(values)
    for offset in range(1, 6):
        slope = slope + deriv_coef[offset - 1] * (
            extended[..., 5 + offset : 5 + offset + columns]
            - extended[..., 5 - offset : 5 - offset + columns]
        )
    mixed = jnp.einsum("ce,belp->bclp", rates, state, preferred_element_type=jnp.float32)
    residual = -speed_in[:, None] * slope - speed_wall[:, None] * normal + density[:, None] * mixed
    return (smooth + section_step * residual).astype(jnp.bfloat16)


def body(
    state,
    speed_in,
    speed_wall,
    density,
    rates,
    wall_op,
    block_perm,
    patch_src,
    patch_flip,
    patch_wall,
):
    owned = state.shape[0]
    rows = state.shape[2]
    gathered = lax.all_gather(edge_cells(state), "blk", axis=0, tiled=True)
    source = source_faces(block_perm, patch_src, patch_wall, lax.axis_index("blk") * owned)
    ghosts = select_ghosts(gathered, source, patch_flip, patch_src.shape[2])
    first_row = lax.axis_index("line") * rows
    my_rows = lax.dynamic_slice_in_dim(wall_op, first_row, rows, 0)
    summed = jnp.einsum(
        "lm,bcmp->bclp",
        my_rows,
        lax.all_gather(state, "line", axis=2, tiled=True),
        preferred_element_type=jnp.float32,
    )
    normal = lax.optimization_barrier(summed.astype(jnp.bfloat16))
    return section_update(
        state, ghosts, normal.astype(jnp.float32), speed_in, speed_wall, density, rates
    )


def solution(mesh):
    return jax.shard_map(
        body,
        mesh=mesh,
        in_specs=(
            P("blk", None, "line", None),
            P("blk", "line", None),
            P("blk", "line", None),
            P("blk", "line", None),
            P(),
            P(),
            P(),
            P("blk", None, "line"),
            P("blk", None, "line"),
            P("blk", None, "line"),
        ),
        out_specs=P("blk", None, "line", None),
        check_vma=False,
    )
```

profile of v0, /device:TPU:0, one launch (start us, length us, event | category | flops | bytes accessed | tf_op | source)
XLA Modules:
  0.0 582.6 jit_solution(9919181915388642683)
XLA Ops:
  6.5 10.9 %fusion.21 = (bf16[4,88,64,5]{3,2,1,0:T(8,128)(2,1)}, bf16[4,88,64,5]{3,2,1,0:T(8,128)(2,1)}) fusion(bf16[4,88,64,128]{3,2,1,0:T(8,128)(2,1)} %param.10), kind=kLoop, calls=%fused_computation.67 | loop fusion | bytes 901120 | tf_op jit(solution)/shard_map/slice | solution.py:15
  17.5 8.2 %copy.32 = bf16[4,88,64,5]{1,2,3,0:T(8,128)(2,1)S(1)} copy(bf16[4,88,64,5]{3,2,1,0:T(8,128)(2,1)} %get-tuple-element.8) | data formatting | bytes 450560
  25.7 8.2 %copy.31 = bf16[4,88,64,5]{1,2,3,0:T(8,128)(2,1)S(1)} copy(bf16[4,88,64,5]{3,2,1,0:T(8,128)(2,1)} %get-tuple-element.7) | data formatting | bytes 450560
  33.9 1.0 pad_maximum_fusion.2
  34.9 0.2 all-gather.5.cloned.1.call-start
  35.1 0.5 all-gather.5.cloned.1.call-update
  35.7 8.2 %convert_element_type.27 = f32[4,88,64,128]{3,2,1,0:T(8,128)} convert(bf16[4,88,64,128]{3,2,1,0:T(8,128)(2,1)} %param.10) | non-fusion elementwise | flops 2883584 | bytes 17301504 | tf_op jit(solution)/shard_map/convert_element_type | solution.py:44
  44.0 0.1 reshape.61
  44.1 0.1 select_reduce_fusion
  44.2 0.7 gather_fusion
  44.9 0.1 reshape.60
  45.0 0.1 bitcast_or_fusion
  45.1 0.1 reshape.67
  45.3 11.3 %fusion.13 = f32[4,64,128,88]{2,3,1,0:T(8,128)} fusion(bf16[4,88,64,128]{3,2,1,0:T(8,128)(2,1)} %param.10, bf16[88,88]{1,0:T(8,128)(2,1)S(1)} %copy-done.4), kind=kOutput, calls=%fused_computation.37 | convolution fusion | flops 507510784 | bytes 17316992 | tf_op jit(solution)/shard_map/ce,belp->bclp/dot_general | solution.py:61
  56.6 22.2 %all-gather.3.cloned.1.call-done = bf16[32,2,88,64,5]{2,3,4,1,0:T(8,128)(2,1)} async-done(((bf16[4,2,88,64,5]{2,3,4,1,0:T(8,128)(2,1)}), bf16[32,2,88,64,5]{2,3,4,1,0:T(8,128)(2,1)}) %all-gather.3.cloned.1.call-update) | async-done | bytes 3604496 | tf_op jit(solution)/shard_map/all_gather | solution.py:80
  78.7 3.2 gather_fusion.1
  82.0 0.8 rev.13
  82.8 0.1 select_bitcast_fusion
  82.9 19.2 %copy.26 = bf16[4,2,88,4,16,5]{5,4,3,2,0,1:T(8,128)(2,1)} copy(bf16[4,2,88,4,16,5]{2,4,5,3,1,0:T(8,128)(2,1)S(1)} %select_bitcast_fusion) | data formatting | bytes 901120 | tf_op jit(solution)/shard_map/transpose | solution.py:39
  102.1 12.3 %fusion.12 = (f32[4,88,64,5]{3,2,1,0:T(8,128)}, f32[4,88,64,5]{3,2,1,0:T(8,128)}) fusion(bf16[4,2,88,64,5]{4,3,2,0,1:T(8,128)(2,1)} %bitcast.45), kind=kLoop, calls=%fused_computation.36 | loop fusion | flops 225280 | bytes 1351680 | tf_op jit(solution)/shard_map/convert_element_type | solution.py:47
  114.4 17.6 %rev.14 = f32[4,88,64,5]{3,2,1,0:T(8,128)} reverse(f32[4,88,64,5]{3,2,1,0:T(8,128)} %get-tuple-element.5), dimensions={3} | reverse | bytes 901120 | tf_op jit(solution)/shard_map/jit(_flip)/rev | solution.py:47
  132.1 339.3 %all-gather.5.cloned.1.call-done = bf16[4,88,256,128]{3,2,1,0:T(8,128)(2,1)} async-done(((bf16[4,88,64,128]{3,2,1,0:T(8,128)(2,1)}), bf16[4,88,256,128]{3,2,1,0:T(8,128)(2,1)}) %all-gather.5.cloned.1.call-update) | async-done | bytes 23068688 | tf_op jit(solution)/shard_map/all_gather | solution.py:88
  471.4 11.7 %convert_bitcast_fusion = bf16[4,88,64,128]{3,2,1,0:T(8,128)(2,1)S(1)} fusion(bf16[4,88,256,128]{3,2,1,0:T(8,128)(2,1)} %all-gather.5.cloned.1.call-done, bf16[256,256]{1,0:T(8,128)(2,1)S(1)} %copy-done, s32[]{:T(128)S(6)} %select_n.47), kind=kOutput, calls=%fused_computation.39 | convolution fusion | flops 1479278592 | bytes 28868612 | tf_op jit(solution)/shard_map/lm,bcmp->bclp/dot_general | solution.py:85
  483.1 92.7 %fusion.10 = bf16[4,88,64,128]{3,2,1,0:T(8,128)(2,1)} fusion(f32[4,64,128,88]{2,3,1,0:T(8,128)} %fusion.13, bf16[4,88,64,128]{3,2,1,0:T(8,128)(2,1)S(1)} %convert_bitcast_fusion, f32[4,88,64,5]{3,2,1,0:T(8,128)} %get-tuple-element.6, f32[4,88,64,128]{3,2,1,0:T(8,128)} %convert_element_type.27, f32[4,88,64,5]{3,2,1,0:T(8,128)} %rev.14, ...), kind=kLoop, calls=%fused_computation.31 | loop fusion | flops 158597120 | bytes 35897344 | tf_op jit(solution)/shard_map/convert_element_type | solution.py:63
  (27 shorter events, 0.2 us)
Async XLA Ops:
  6.5 464.9 %copy-start = (bf16[256,256]{1,0:T(8,128)(2,1)S(1)}, bf16[256,256]{1,0:T(8,128)(2,1)}, u32[]{:S(2)}) copy-start(bf16[256,256]{1,0:T(8,128)(2,1)} %param.15) | copy-start | bytes 393220
  6.5 72.2 %all-gather.3.cloned.1.call-start = ((), (), s32[]{:S(2)}) async-start(), calls=%async_computation | async-start | bytes 5898240 | tf_op jit(solution)/shard_map/all_gather | solution.py:80
  34.9 9.1 %copy-start.5 = (s32[4,2,4]{2,1,0:T(2,128)S(1)}, s32[4,2,4]{2,1,0:T(2,128)}, u32[]{:S(2)}) copy-start(s32[4,2,4]{2,1,0:T(2,128)} %param.17) | copy-start | bytes 388
  34.9 9.2 %copy-start.8 = (s32[32]{0:T(128)S(1)}, s32[32]{0:T(128)}, u32[]{:S(2)}) copy-start(s32[32]{0:T(128)} %param.16) | copy-start | bytes 388
  34.9 436.5 %all-gather.5.cloned.1.call-start = ((), (), s32[]{:S(2)}) async-start(), calls=%async_computation.1 | async-start | bytes 28835840 | tf_op jit(solution)/shard_map/all_gather | solution.py:88
  35.6 9.4 %copy-start.7 = (s32[4,2,4]{2,1,0:T(2,128)S(1)}, s32[4,2,4]{2,1,0:T(2,128)}, u32[]{:S(2)}) copy-start(s32[4,2,4]{2,1,0:T(2,128)} %param.19) | copy-start | bytes 388
  35.7 9.6 %copy-start.3 = (f32[4,64,128]{2,1,0:T(8,128)S(1)}, f32[4,64,128]{2,1,0:T(8,128)}, u32[]{:S(2)}) copy-start(f32[4,64,128]{2,1,0:T(8,128)} %param.11) | copy-start | bytes 393220
  35.7 9.6 %copy-start.6 = (s32[4,2,4]{2,1,0:T(2,128)S(1)}, s32[4,2,4]{2,1,0:T(2,128)}, u32[]{:S(2)}) copy-start(s32[4,2,4]{2,1,0:T(2,128)} %param.18) | copy-start | bytes 388
  35.7 9.6 %copy-start.4 = (bf16[88,88]{1,0:T(8,128)(2,1)S(1)}, bf16[88,88]{1,0:T(8,128)(2,1)}, u32[]{:S(2)}) copy-start(bf16[88,88]{1,0:T(8,128)(2,1)} %param.14) | copy-start | bytes 46468
  132.1 351.0 %copy-start.1 = (f32[4,64,128]{2,1,0:T(8,128)S(1)}, f32[4,64,128]{2,1,0:T(8,128)}, u32[]{:S(2)}) copy-start(f32[4,64,128]{2,1,0:T(8,128)} %param.13) | copy-start | bytes 393220
  132.1 351.0 %copy-start.2 = (f32[4,64,128]{2,1,0:T(8,128)S(1)}, f32[4,64,128]{2,1,0:T(8,128)}, u32[]{:S(2)}) copy-start(f32[4,64,128]{2,1,0:T(8,128)} %param.12) | copy-start | bytes 393220
Sparse Core Ops, SparseCore 0:
  35.0 43.6 all-gather.2
  80.3 391.0 all-gather.4
where the time goes:
time: 583 us
  waiting for transfers between devices  362 us (62%)
  other arithmetic  115 us (20%)
  local copies, waits for them, and re-layouts  69.1 us (12%)
  matrix products  23 us (4%)
  between operations  13.6 us (2%)
    all_gather x1, waiting for transfers between devices, body(): lax.all_gather(state, 'line', axis=2, tiled=True)  339 us
    convert_element_type x1, other arithmetic, section_update(): return (smooth + section_step * residual).astype(jnp.bfloat16)  92.7 us
    all_gather x1, waiting for transfers between devices, body(): gathered = lax.all_gather(edge_cells(state), 'blk', axis=0, tiled=True)  22.2 us
    transpose x1, local copies, waits for them, and re-layouts, select_ghosts(): picked = jnp.transpose(picked, (0, 1, 3, 2, 4, 5))  19.2 us
    rev x1, local copies, waits for them, and re-layouts, section_update(): jnp.flip(ghosts[:, 0].astype(jnp.float32), -1)  17.6 us
    unnamed x20, local copies, waits for them, and re-layouts  16.4 us
    convert_element_type x1, other arithmetic, section_update(): ghosts[:, 0].astype(jnp.float32)  12.3 us
    dot_general x1, matrix products, body(): jnp.einsum('lm,bcmp->bclp', my_rows, lax.all_gather(state, 'line', axis=2...  11.7 us
  transfers between devices with their start and end apart: 2, of which 2 were waited for; matrix products, arithmetic and copies ran while one was open for 13% of the time, Pallas kernels for 0%

commit v1 on v0

--- a/solution.py
+++ b/solution.py
@@ -8,6 +8,26 @@
 section_step = 0.25
 deriv_coef = [5.0 / 6.0, -5.0 / 21.0, 5.0 / 84.0, -5.0 / 504.0, 1.0 / 1260.0]
 high_pass = [(-1) ** offset * math.comb(10, 5 + offset) / 1024.0 for offset in range(-5, 6)]
+
+
+def bind_gates(s0, bus_axis, chunk):
+    built, right_arr, local_part = (
+        jax.lax.axis_size(bus_axis),
+        jax.lax.axis_index(bus_axis),
+        s0.shape[2],
+    )
+    copies = tuple(((it, (it + 1) % built) for it in range(built)))
+    heap = tuple(((it, (it - 1) % built) for it in range(built)))
+    all_rows = built // 2
+    state_now = y2 = s0
+    shaped = chunk(s0, right_arr * local_part)
+    for j in range(1, all_rows + 1):
+        state_now = jax.lax.ppermute(state_now, bus_axis, perm=copies)
+        if j < built - all_rows:
+            y2 = jax.lax.ppermute(y2, axis_name=bus_axis, perm=heap)
+            shaped = shaped + chunk(y2, (right_arr + j) % built * local_part)
+        shaped = shaped + chunk(state_now, (right_arr - j) % built * local_part)
+    return shaped
 
 
 def edge_cells(field):
@@ -82,11 +102,15 @@
     ghosts = select_ghosts(gathered, source, patch_flip, patch_src.shape[2])
     first_row = lax.axis_index("line") * rows
     my_rows = lax.dynamic_slice_in_dim(wall_op, first_row, rows, 0)
-    summed = jnp.einsum(
-        "lm,bcmp->bclp",
-        my_rows,
-        lax.all_gather(state, "line", axis=2, tiled=True),
-        preferred_element_type=jnp.float32,
+    summed = bind_gates(
+        state,
+        bus_axis="line",
+        chunk=lambda part, offset_2: jnp.einsum(
+            "lm,bcmp->bclp",
+            lax.dynamic_slice_in_dim(my_rows, offset_2, part.shape[2], axis=1),
+            part,
+            preferred_element_type=jnp.float32,
+        ),
     )
     normal = lax.optimization_barrier(summed.astype(jnp.bfloat16))
     return section_update(

time: 583 us -> 505 us (0.87)
  waiting for transfers between devices: 362 us -> 246 us
  matrix products: 23 us -> 51.2 us
    all_gather x1 -> x0, waiting for transfers between devices: 339 us -> none  [body(): lax.all_gather(state, 'line', axis=2, tiled=True)]
    ppermute x0 -> x3, waiting for transfers between devices: none -> 246 us  [the longest x2 160 us: bind_gates(): state_now = jax.lax.ppermute(state_now, bus_axis, perm=copies)]
    dot_general x1 -> x4, matrix products: 11.7 us -> 42.7 us  [body(): jnp.einsum('lm,bcmp->bclp', lax.dynamic_slice_in_dim(my_rows, offset_2, p...]
    all_gather x1, waiting for transfers between devices: 22.2 us -> 0.01 us  [body(): gathered = lax.all_gather(edge_cells(state), 'blk', axis=0, tiled=True)]
    unnamed x20 -> x24, local copies, waits for them, and re-layouts: 16.4 us -> 16.4 us
  transfers between devices with their start and end apart: 2 -> 4, of which waited for: 2 -> 3; matrix products, arithmetic and copies ran while one was open for 13% -> 25% of each run, Pallas kernels for 0% -> 0%
where the time goes in v1:
time: 505 us; the launch traced here: 504 us
  waiting for transfers between devices  246 us (49%)
  other arithmetic  119 us (24%)
  local copies, waits for them, and re-layouts  69.1 us (14%)
  matrix products  51.2 us (10%)
  between operations  13.6 us (3%)
  starting transfers between devices  5.09 us (1%)
    ppermute x2, waiting for transfers between devices, bind_gates(): state_now = jax.lax.ppermute(state_now, bus_axis, perm=copies)  160 us
    convert_element_type x1, other arithmetic, section_update(): return (smooth + section_step * residual).astype(jnp.bfloat16)  97.2 us
    ppermute x1, waiting for transfers between devices, bind_gates(): y2 = jax.lax.ppermute(y2, axis_name=bus_axis, perm=heap)  86.9 us
    dot_general x4, matrix products, body(): jnp.einsum('lm,bcmp->bclp', lax.dynamic_slice_in_dim(my_rows, offset_2, p...  42.7 us
    transpose x1, local copies, waits for them, and re-layouts, select_ghosts(): picked = jnp.transpose(picked, (0, 1, 3, 2, 4, 5))  19.2 us
    rev x1, local copies, waits for them, and re-layouts, section_update(): jnp.flip(ghosts[:, 0].astype(jnp.float32), -1)  17.6 us
    unnamed x24, local copies, waits for them, and re-layouts  16.4 us
    convert_element_type x1, other arithmetic, section_update(): ghosts[:, 0].astype(jnp.float32)  12 us
  transfers between devices with their start and end apart: 4, of which 3 were waited for; matrix products, arithmetic and copies ran while one was open for 25% of the time, Pallas kernels for 0%

profile of v1, /device:TPU:0, one launch (start us, length us, event | category | flops | bytes accessed | tf_op | source)
XLA Modules:
  0.0 504.4 jit_solution(12324888717607153495)
XLA Ops:
  6.5 3.1 collective-permute-start.1
  9.6 2.0 collective-permute-start
  11.6 10.9 %fusion.30 = (bf16[4,88,64,5]{3,2,1,0:T(8,128)(2,1)}, bf16[4,88,64,5]{3,2,1,0:T(8,128)(2,1)}) fusion(bf16[4,88,64,128]{3,2,1,0:T(8,128)(2,1)} %param.10), kind=kLoop, calls=%fused_computation.76 | loop fusion | bytes 901120 | tf_op jit(solution)/shard_map/slice | solution.py:35
  22.6 8.2 %copy.35 = bf16[4,88,64,5]{1,2,3,0:T(8,128)(2,1)S(1)} copy(bf16[4,88,64,5]{3,2,1,0:T(8,128)(2,1)} %get-tuple-element.8) | data formatting | bytes 450560
  30.7 8.2 %copy.34 = bf16[4,88,64,5]{1,2,3,0:T(8,128)(2,1)S(1)} copy(bf16[4,88,64,5]{3,2,1,0:T(8,128)(2,1)} %get-tuple-element.7) | data formatting | bytes 450560
  39.0 1.0 pad_maximum_fusion.2
  40.0 97.1 %collective-permute-done.1 = bf16[4,88,64,128]{3,2,1,0:T(8,128)(2,1)} collective-permute-done((bf16[4,88,64,128]{3,2,1,0:T(8,128)(2,1)}, bf16[4,88,64,128]{3,2,1,0:T(8,128)(2,1)}, u32[]{:S(2)}, u32[]{:S(2)}) %collective-permute-start.1) | collective-permute-done | bytes 5767200 | tf_op jit(solution)/shard_map/ppermute | solution.py:25
  137.1 8.4 %convert_element_type.27 = f32[4,88,64,128]{3,2,1,0:T(8,128)} convert(bf16[4,88,64,128]{3,2,1,0:T(8,128)(2,1)} %param.10) | non-fusion elementwise | flops 2883584 | bytes 17301504 | tf_op jit(solution)/shard_map/convert_element_type | solution.py:64
  145.6 0.1 select_reduce_fusion
  145.7 0.7 gather_fusion
  146.8 8.7 %fusion.22 = f32[64,4,88,128]{3,0,2,1:T(8,128)} fusion(bf16[4,88,64,128]{3,2,1,0:T(8,128)(2,1)} %param.10, bf16[256,256]{1,0:T(8,128)(2,1)S(1)} %copy-done, s32[]{:T(128)S(6)} %select_n.80), kind=kOutput, calls=%fused_computation.50 | convolution fusion | flops 369098752 | bytes 17317892 | tf_op jit(solution)/shard_map/lm,bcmp->bclp/dot_general | solution.py:108
  155.6 8.5 %fusion.14 = f32[4,64,128,88]{2,3,1,0:T(8,128)} fusion(bf16[4,88,64,128]{3,2,1,0:T(8,128)(2,1)S(1)} %bitcast.64, bf16[88,88]{1,0:T(8,128)(2,1)S(1)} %copy-done.4), kind=kOutput, calls=%fused_computation.39 | convolution fusion | flops 507510784 | bytes 17316992 | tf_op jit(solution)/shard_map/ce,belp->bclp/dot_general | solution.py:81
  164.1 8.5 %fusion.18 = f32[64,4,88,128]{3,0,2,1:T(8,128)} fusion(bf16[4,88,64,128]{3,2,1,0:T(8,128)(2,1)} %collective-permute-done.1, bf16[256,256]{1,0:T(8,128)(2,1)S(1)} %copy-done, s32[]{:T(128)S(6)} %select_n.80, s32[]{:T(128)S(6)} %select_n.86), kind=kOutput, calls=%fused_computation.46 | convolution fusion | flops 369098752 | bytes 17317896 | tf_op jit(solution)/shard_map/lm,bcmp->bclp/dot_general | solution.py:108
  172.6 86.9 %collective-permute-done = bf16[4,88,64,128]{3,2,1,0:T(8,128)(2,1)} collective-permute-done((bf16[4,88,64,128]{3,2,1,0:T(8,128)(2,1)}, bf16[4,88,64,128]{3,2,1,0:T(8,128)(2,1)}, u32[]{:S(2)}, u32[]{:S(2)}) %collective-permute-start) | collective-permute-done | bytes 5767200 | tf_op jit(solution)/shard_map/ppermute | solution.py:27
  259.5 8.5 %fusion.20 = f32[64,4,88,128]{3,0,2,1:T(8,128)} fusion(bf16[4,88,64,128]{3,2,1,0:T(8,128)(2,1)} %collective-permute-done, bf16[256,256]{1,0:T(8,128)(2,1)S(1)} %copy-done, s32[]{:T(128)S(6)} %select_n.80, s32[]{:T(128)S(6)} %select_n.83), kind=kOutput, calls=%fused_computation.48 | convolution fusion | flops 369098752 | bytes 17317896 | tf_op jit(solution)/shard_map/lm,bcmp->bclp/dot_general | solution.py:108
  268.0 3.2 gather_fusion.1
  271.2 0.8 rev.13
  272.0 0.1 select_bitcast_fusion
  272.2 19.2 %copy.26 = bf16[4,2,88,4,16,5]{5,4,3,2,0,1:T(8,128)(2,1)} copy(bf16[4,2,88,4,16,5]{2,4,5,3,1,0:T(8,128)(2,1)S(1)} %select_bitcast_fusion) | data formatting | bytes 901120 | tf_op jit(solution)/shard_map/transpose | solution.py:59
  291.4 12.0 %fusion.13 = (f32[4,88,64,5]{3,2,1,0:T(8,128)}, f32[4,88,64,5]{3,2,1,0:T(8,128)}) fusion(bf16[4,2,88,64,5]{4,3,2,0,1:T(8,128)(2,1)} %bitcast.65), kind=kLoop, calls=%fused_computation.38 | loop fusion | flops 225280 | bytes 1351680 | tf_op jit(solution)/shard_map/convert_element_type | solution.py:67
  303.4 17.6 %rev.14 = f32[4,88,64,5]{3,2,1,0:T(8,128)} reverse(f32[4,88,64,5]{3,2,1,0:T(8,128)} %get-tuple-element.5), dimensions={3} | reverse | bytes 901120 | tf_op jit(solution)/shard_map/jit(_flip)/rev | solution.py:67
  321.0 62.5 %collective-permute-done.2 = bf16[4,88,64,128]{3,2,1,0:T(8,128)(2,1)} collective-permute-done((bf16[4,88,64,128]{3,2,1,0:T(8,128)(2,1)}, bf16[4,88,64,128]{3,2,1,0:T(8,128)(2,1)}, u32[]{:S(2)}, u32[]{:S(2)}) %collective-permute-start.2) | collective-permute-done | bytes 5767200 | tf_op jit(solution)/shard_map/ppermute | solution.py:25
  383.4 17.0 %fusion.11 = bf16[4,88,64,128]{3,2,1,0:T(8,128)(2,1)} fusion(f32[64,4,88,128]{3,0,2,1:T(8,128)} %fusion.18, f32[64,4,88,128]{3,0,2,1:T(8,128)} %fusion.22, f32[64,4,88,128]{3,0,2,1:T(8,128)} %fusion.20, bf16[4,88,64,128]{3,2,1,0:T(8,128)(2,1)} %collective-permute-done.2, bf16[256,256]{1,0:T(8,128)(2,1)S(1)} %copy-done, s32[]{:T(128)S(6)} %select_n.80, ...), kind=kOutput, calls=%fused_computation.34 | convolution fusion | flops 380633088 | bytes 46153736 | tf_op jit(solution)/shard_map/lm,bcmp->bclp/dot_general | solution.py:108
  400.4 97.2 %fusion.10 = bf16[4,88,64,128]{3,2,1,0:T(8,128)(2,1)} fusion(f32[4,64,128,88]{2,3,1,0:T(8,128)} %fusion.14, bf16[4,88,64,128]{3,2,1,0:T(8,128)(2,1)} %fusion.11, f32[4,88,64,5]{3,2,1,0:T(8,128)} %get-tuple-element.6, f32[4,88,64,128]{3,2,1,0:T(8,128)} %convert_element_type.27, f32[4,88,64,5]{3,2,1,0:T(8,128)} %rev.14, f32[4,64,128]{2,1,0:T(8,128)S(1)} %copy-done.1, ...), kind=kLoop, calls=%fused_computation.31 | loop fusion | flops 158597120 | bytes 35897344 | tf_op jit(solution)/shard_map/convert_element_type | solution.py:83
  (38 shorter events, 0.6 us)
Async XLA Ops:
  6.5 140.3 %copy-start = (bf16[256,256]{1,0:T(8,128)(2,1)S(1)}, bf16[256,256]{1,0:T(8,128)(2,1)}, u32[]{:S(2)}) copy-start(bf16[256,256]{1,0:T(8,128)(2,1)} %param.15) | copy-start | bytes 393220
  6.5 261.5 %all-gather.2.cloned.1.call-start = ((), (), s32[]{:S(2)}) async-start(), calls=%async_computation | async-start | bytes 5898240 | tf_op jit(solution)/shard_map/all_gather | solution.py:100
  6.5 130.6 %collective-permute-start.1 = (bf16[4,88,64,128]{3,2,1,0:T(8,128)(2,1)}, bf16[4,88,64,128]{3,2,1,0:T(8,128)(2,1)}, u32[]{:S(2)}, u32[]{:S(2)}) collective-permute-start(bf16[4,88,64,128]{3,2,1,0:T(8,128)(2,1)} %param.10), channel_id=1, source_target_pairs={{0,1},{1,2},{2,3},{3,0},{4,5},{5,6},{6,7},{7,4},{8,9},{9,10},{10,1... | collective-permute-start | bytes 17301512 | tf_op jit(solution)/shard_map/ppermute | solution.py:25
  9.6 249.9 %collective-permute-start = (bf16[4,88,64,128]{3,2,1,0:T(8,128)(2,1)}, bf16[4,88,64,128]{3,2,1,0:T(8,128)(2,1)}, u32[]{:S(2)}, u32[]{:S(2)}) collective-permute-start(bf16[4,88,64,128]{3,2,1,0:T(8,128)(2,1)} %param.10), channel_id=1, source_target_pairs={{0,3},{1,0},{2,1},{3,2},{4,7},{5,4},{6,5},{7,6},{8,11},{9,8},{10,9... | collective-permute-start | bytes 17301512 | tf_op jit(solution)/shard_map/ppermute | solution.py:27
  38.9 106.6 %copy-start.5 = (s32[4,2,4]{2,1,0:T(2,128)S(1)}, s32[4,2,4]{2,1,0:T(2,128)}, u32[]{:S(2)}) copy-start(s32[4,2,4]{2,1,0:T(2,128)} %param.17) | copy-start | bytes 388
  38.9 106.7 %copy-start.8 = (s32[32]{0:T(128)S(1)}, s32[32]{0:T(128)}, u32[]{:S(2)}) copy-start(s32[32]{0:T(128)} %param.16) | copy-start | bytes 388
  39.0 107.6 %copy-start.7 = (s32[4,2,4]{2,1,0:T(2,128)S(1)}, s32[4,2,4]{2,1,0:T(2,128)}, u32[]{:S(2)}) copy-start(s32[4,2,4]{2,1,0:T(2,128)} %param.19) | copy-start | bytes 388
  39.0 107.8 %copy-start.3 = (f32[4,64,128]{2,1,0:T(8,128)S(1)}, f32[4,64,128]{2,1,0:T(8,128)}, u32[]{:S(2)}) copy-start(f32[4,64,128]{2,1,0:T(8,128)} %param.11) | copy-start | bytes 393220
  40.0 106.8 %copy-start.6 = (s32[4,2,4]{2,1,0:T(2,128)S(1)}, s32[4,2,4]{2,1,0:T(2,128)}, u32[]{:S(2)}) copy-start(s32[4,2,4]{2,1,0:T(2,128)} %param.18) | copy-start | bytes 388
  137.1 246.3 %collective-permute-start.2 = (bf16[4,88,64,128]{3,2,1,0:T(8,128)(2,1)}, bf16[4,88,64,128]{3,2,1,0:T(8,128)(2,1)}, u32[]{:S(2)}, u32[]{:S(2)}) collective-permute-start(bf16[4,88,64,128]{3,2,1,0:T(8,128)(2,1)} %collective-permute-done.1), channel_id=1, source_target_pairs={{0,1},{1,2},{2,3},{3,0},{4,5},{5,6},{6,7},{7,4},{8,9},{9,10},{10,1... | collective-permute-start | bytes 17301512 | tf_op jit(solution)/shard_map/ppermute | solution.py:25
  145.5 10.1 %slice-start = ((s8[5767168]{0:T(1024)(128)(4,1)}), s8[1572864]{0:T(1024)(128)(4,1)S(1)}, s32[]{:S(2)}) async-start(s8[5767168]{0:T(1024)(128)(4,1)} %bitcast.63), calls=%async_computation.1 | async-start | bytes 3145728
  145.5 10.1 %copy-start.4 = (bf16[88,88]{1,0:T(8,128)(2,1)S(1)}, bf16[88,88]{1,0:T(8,128)(2,1)}, u32[]{:S(2)}) copy-start(bf16[88,88]{1,0:T(8,128)(2,1)} %param.14) | copy-start | bytes 46468
  146.8 8.7 %slice-start.1 = ((s8[5767168]{0:T(1024)(128)(4,1)}), s8[4194304]{0:T(1024)(128)(4,1)S(1)}, s32[]{:S(2)}) async-start(s8[5767168]{0:T(1024)(128)(4,1)} %bitcast.63), calls=%async_computation.2 | async-start | bytes 8388608
  321.0 79.4 %copy-start.1 = (f32[4,64,128]{2,1,0:T(8,128)S(1)}, f32[4,64,128]{2,1,0:T(8,128)}, u32[]{:S(2)}) copy-start(f32[4,64,128]{2,1,0:T(8,128)} %param.13) | copy-start | bytes 393220
  321.0 79.4 %copy-start.2 = (f32[4,64,128]{2,1,0:T(8,128)S(1)}, f32[4,64,128]{2,1,0:T(8,128)}, u32[]{:S(2)}) copy-start(f32[4,64,128]{2,1,0:T(8,128)} %param.12) | copy-start | bytes 393220
Sparse Core Ops, SparseCore 0:
  40.1 40.6 all-gather.1
